TPU v7x, 512 devices: a whole 4x4x16 slice. The times are simulated.
512 devices in a mesh: row: 32 (over x, z_hi, core), col: 16 (over z_lo, y).
Axes of the slice: x: 4, y: 4, z: 16 (z_hi: 4, z_lo: 4; z = z_hi * 4 + z_lo), core: 2. Of those that a mesh axis runs over, the one named last changes fastest.
Arguments:
- top_inverse: float32 [2, 4096, 4096], P(None, 'row', 'col'), may hold values from -6 to 6
- panel: float32 [2, 2048, 8192], P(None, 'row', 'col'), may hold values from -0.09375 to 0.09375
- leaf_rows: int32 [32, 8], P('col'), may hold values from 0 to 15, as said below
- leaf_counts: int32 [32], P('col'), may hold values from 1 to 8, as said below
- diag_inverse: float32 [2, 256, 8192], P(None, 'row', 'col'), may hold values from -6 to 6
Outputs:
- selected: float32 [2, 4096, 8192], P(None, 'row', 'col')
- diagonal: float32 [2, 256, 8192], P(None, 'row', 'col')
Inputs may be any that keep to these rules, and one draw needn't show every extreme that they name: `leaf_rows`: the 8 entries of each leaf are distinct separator blocks. Slots 0 to leaf_counts - 1 of a leaf are live.
All inputs are finite; a program needn't handle non-finite values.
Results may differ from a plain program's by a relative error of at most 0.0003.
Values sent between devices are 32-bit elements; how exact they have to be, the bound alone decides.
A program may use at most 128 MiB of HBM per device.

v0:
```python
import jax
import jax.numpy as jnp
from jax import lax
from jax.sharding import PartitionSpec as P

B = 256
ROW_DEV = 128
LEAF_COL = 2


def product_highest(left, right):
    return jnp.dot(left, right, precision=lax.Precision.HIGHEST, preferred_element_type=jnp.float32)


def complex_product(left_real, left_imag, right_real, right_imag):
    real_part = product_highest(left_real, right_real) - product_highest(left_imag, right_imag)
    imag_part = product_highest(left_real, right_imag) + product_highest(left_imag, right_real)
    return (real_part, imag_part)


def on_device(top_inverse, panel, leaf_rows, leaf_counts, diag_inverse):
    slot_count = leaf_rows.shape[1]
    row_index = lax.axis_index("row")
    first_row = row_index * ROW_DEV
    my_block = first_row // B
    offset = first_row % B
    active_slots = jnp.arange(slot_count, dtype=jnp.int32)[None, :] < leaf_counts[:, None]
    block_live = jnp.any((leaf_rows == my_block) & active_slots, axis=1)
    targets = jnp.arange(ROW_DEV, dtype=jnp.int32)
    top_strip = lax.all_gather(top_inverse, "col", axis=2, tiled=True)
    section = lax.all_gather(panel, "row", axis=1, tiled=True)
    length = section.shape[1]
    gains_prod = []
    gains_low = []
    for absorb_member in range(LEAF_COL):
        position = jnp.arange(length, dtype=jnp.int32)
        slot_index = position // B
        slot_within = position % B
        slot_target_block = jnp.take(leaf_rows[absorb_member], slot_index)
        slot_active = slot_index < leaf_counts[absorb_member]
        columns = slot_target_block * B + slot_within
        panel_part = (
            section[:, :, absorb_member * B : (absorb_member + 1) * B]
            * slot_active.astype(jnp.float32)[None, :, None]
        )
        picked = jnp.take(top_strip, columns, axis=2)
        real_part, imag_part = complex_product(picked[0], picked[1], panel_part[0], panel_part[1])
        gain_prod = jnp.stack([real_part, imag_part])
        owned = slot_active & (slot_target_block == my_block)
        select = ((slot_within[None, :] - offset == targets[:, None]) & owned[None, :]).astype(
            jnp.float32
        )
        gain_low = jnp.stack(
            [product_highest(select, panel_part[0]), product_highest(select, panel_part[1])]
        )
        gains_prod.append(gain_prod)
        gains_low.append(gain_low)
    product = jnp.concatenate(gains_prod, axis=2)
    lower_rows = jnp.concatenate(gains_low, axis=2)
    keep_rows = jnp.repeat(block_live.astype(jnp.float32), B)
    selected = -product * keep_rows[None, None, :]
    diag_parts = []
    for member in range(LEAF_COL):
        sel_block = selected[:, :, member * B : (member + 1) * B]
        low_block = lower_rows[:, :, member * B : (member + 1) * B]
        diag_real, diag_imag = complex_product(
            sel_block[0].T, sel_block[1].T, low_block[0], low_block[1]
        )
        diag_parts.append(jnp.stack([diag_real, diag_imag]))
    partial_diag = jnp.concatenate(diag_parts, axis=2)
    total_sum = lax.psum(partial_diag, "row")
    share_rows = diag_inverse.shape[1]
    share_sum = lax.dynamic_slice_in_dim(total_sum, row_index * share_rows, share_rows, 1)
    return (selected, diag_inverse - share_sum)


def solution(mesh):
    return jax.shard_map(
        on_device,
        mesh=mesh,
        in_specs=(
            P(None, "row", "col"),
            P(None, "row", "col"),
            P("col", None),
            P("col"),
            P(None, "row", "col"),
        ),
        out_specs=(P(None, "row", "col"), P(None, "row", "col")),
        check_vma=False,
    )
```

profile of v0, /device:TPU:1, one launch (start us, length us, event | category | flops | bytes accessed | tf_op | source)
XLA Modules:
  0.0 626.7 jit_solution(4336711945029545441)
XLA Ops:
  7.2 0.0 all-gather.3.cloned.1.call-start
  7.2 1.8 copy.12
  9.0 0.0 all-gather.3.cloned.1.call-update
  9.0 0.0 all-gather.5.cloned.1.call-start
  9.1 0.7 all-gather.5.cloned.1.call-update
  9.8 0.0 all-reduce.2.cloned.1.call-start
  9.8 0.9 and_reduce_fusion
  10.7 0.1 broadcast_bitcast_fusion
  10.8 0.8 slice_bitcast_fusion.45
  11.6 0.7 fusion.70
  12.3 5.2 compare_and_fusion.1
  17.4 1.4 fusion.69
  18.8 5.7 compare_and_fusion.3
  24.5 4.9 compare_and_fusion
  29.4 5.5 compare_and_fusion.2
  35.0 4.9 broadcast_clamp_fusion
  39.9 5.2 broadcast_clamp_fusion.1
  45.1 1.2 fusion.65
  46.3 52.9 %all-gather.3.cloned.1.call-done = f32[2,128,4096]{1,0,2:T(2,128)} async-done(((f32[2,128,256]{1,0,2:T(2,128)}), f32[2,128,4096]{1,0,2:T(2,128)}) %all-gather.3.cloned.1.call-update) | async-done | bytes 4194320 | tf_op jit(solution)/shard_map/all_gather | solution.py:30
  99.2 9.0 %gather_fusion.1 = f32[2048,2,128]{2,1,0:T(2,128)S(1)} fusion(f32[2,128,4096]{1,0,2:T(2,128)} %all-gather.3.cloned.1.call-done, s32[2048]{0:T(1024)S(1)} %broadcast_clamp_fusion), kind=kCustom, calls=%fused_computation.1.clone | custom fusion | bytes 4202496 | tf_op jit(solution)/shard_map/jit(_take)/gather | solution.py:46
  108.2 16.7 %gather_fusion = f32[2048,2,128]{2,1,0:T(2,128)} fusion(f32[2,128,4096]{1,0,2:T(2,128)} %all-gather.3.cloned.1.call-done, s32[2048]{0:T(1024)S(1)} %broadcast_clamp_fusion.1), kind=kCustom, calls=%fused_computation.clone | custom fusion | bytes 4202496 | tf_op jit(solution)/shard_map/jit(_take)/gather | solution.py:46
  124.9 7.4 %select_bitcast_fusion = f32[2,128,2048]{1,0,2:T(2,128)S(1)} fusion(f32[2048,2,128]{2,1,0:T(2,128)S(1)} %gather_fusion.1, pred[2048]{0:T(1024)(128)(4,1)S(1)} %compare_and_fusion), kind=kLoop, calls=%fused_computation.8 | loop fusion | flops 524288 | bytes 4196352 | tf_op jit(solution)/shard_map/jit(_take)/select_n | solution.py:46
  132.3 0.0 copy-start.1
  132.3 1.7 fusion.68
  134.0 0.0 copy-done.1
  134.0 7.4 %select_bitcast_fusion.1 = f32[2,128,2048]{1,0,2:T(2,128)S(1)} fusion(f32[2048,2,128]{2,1,0:T(2,128)S(1)} %copy-done.1, pred[2048]{0:T(1024)(128)(4,1)S(1)} %compare_and_fusion.1), kind=kLoop, calls=%fused_computation.9 | loop fusion | flops 524288 | bytes 4196352 | tf_op jit(solution)/shard_map/jit(_take)/select_n | solution.py:46
  141.5 2.5 fusion.67
  144.0 102.6 %all-gather.5.cloned.1.call-done = f32[2,2048,512]{2,1,0:T(8,128)} async-done(((f32[2,64,512]{2,1,0:T(8,128)}), f32[2,2048,512]{2,1,0:T(8,128)}) %all-gather.5.cloned.1.call-update) | async-done | bytes 8388624 | tf_op jit(solution)/shard_map/all_gather | solution.py:31
  246.6 4.1 slice_multiply_fusion.1
  250.7 1.0 fusion.3
  251.7 1.0 fusion
  252.7 1.0 fusion.9
  253.7 1.0 fusion.6
  254.8 0.0 copy-start
  254.8 1.9 fusion.1
  256.6 0.0 copy-done
  256.6 1.9 fusion.2
  258.6 1.9 fusion.23
  260.5 1.9 fusion.21
  262.4 2.1 fusion.7
  264.5 1.9 fusion.8
  266.3 1.9 fusion.19
  268.2 1.9 fusion.17
  270.1 0.1 fusion.30
  270.1 0.0 copy-start.2
  270.1 0.4 fusion.41
  270.6 0.4 fusion.42
  271.0 0.4 fusion.12
  271.4 0.4 fusion.13
  271.8 0.4 fusion.39
  272.3 0.4 fusion.40
  272.7 0.4 fusion.14
  273.1 0.0 copy-done.2
  273.1 0.0 copy-start.3
  273.1 0.4 fusion.15
  273.5 1.1 maximum_maximum_fusion
  274.6 0.0 all-reduce.2.cloned.1.call-update
  274.6 0.0 copy-done.3
  274.7 0.2 copy.13
  274.9 343.3 %all-reduce.2.cloned.1.call-done = f32[2,256,512]{1,2,0:T(8,128)} async-done(((f32[2,256,512]{1,2,0:T(8,128)}), f32[2,256,512]{1,2,0:T(8,128)}) %all-reduce.2.cloned.1.call-update) | async-done | bytes 1048592 | tf_op jit(solution)/shard_map/psum | solution.py:71
  618.2 1.2 dynamic-slice_subtract_fusion
  619.4 0.8 copy.14
  (3 shorter events, 0.0 us)
Async XLA Ops:
  7.2 92.1 %all-gather.3.cloned.1.call-start = ((), (), s32[]{:S(2)}) async-start(), calls=%async_computation | async-start | bytes 4456448 | tf_op jit(solution)/shard_map/all_gather | solution.py:30
  9.0 237.5 %all-gather.5.cloned.1.call-start = ((), (), s32[]{:S(2)}) async-start(), calls=%async_computation.1 | async-start | bytes 8650752 | tf_op jit(solution)/shard_map/all_gather | solution.py:31
  9.8 608.4 %all-reduce.2.cloned.1.call-start = ((), (), s32[]{:S(2)}) async-start(), calls=%async_computation.2 | async-start | bytes 2097152 | tf_op jit(solution)/shard_map/psum | solution.py:71
  132.3 1.7 copy-start.1
  254.8 1.9 copy-start
  270.1 3.0 copy-start.2
  273.1 1.5 copy-start.3
Sparse Core Ops, SparseCore 0:
  10.6 88.5 all-gather.2
  102.5 144.0 all-gather.4
  274.8 343.3 all-reduce.1
where the time goes:
time: 627 us
  waiting for transfers between devices  500 us (80%)
  other arithmetic  54.8 us (9%)
  local copies, waits for them, and re-layouts  35.5 us (6%)
  matrix products  22.6 us (4%)
  between operations  14.1 us (2%)
    psum x1, waiting for transfers between devices, on_device(): total_sum = lax.psum(partial_diag, 'row')  343 us
    all_gather x1, waiting for transfers between devices, on_device(): section = lax.all_gather(panel, 'row', axis=1, tiled=True)  103 us
    all_gather x1, waiting for transfers between devices, on_device(): top_strip = lax.all_gather(top_inverse, 'col', axis=2, tiled=True)  52.9 us
    gather x2, local copies, waits for them, and re-layouts, on_device(): picked = jnp.take(top_strip, columns, axis=2)  25.6 us
    dot_general x20, matrix products, product_highest(): jnp.dot(left, right, precision=lax.Precision.HIGHEST, preferred_element_t...  22.6 us
    select_n x2, other arithmetic, on_device(): picked = jnp.take(top_strip, columns, axis=2)  14.9 us
  transfers between devices with their start and end apart: 3, of which 3 were waited for; matrix products, arithmetic and copies ran while one was open for 13% of the time, Pallas kernels for 0%

commit v1 on v0

--- a/solution.py
+++ b/solution.py
@@ -6,6 +6,10 @@
 B = 256
 ROW_DEV = 128
 LEAF_COL = 2
+set_side = lambda my_data, pos_dim: jnp.concatenate(
+    jax.lax.all_to_all(jnp.stack([my_data for _ in range(jax.lax.axis_size("col"))]), "col", 0, 0),
+    axis=pos_dim,
+)
 
 
 def product_highest(left, right):
@@ -27,7 +31,7 @@
     active_slots = jnp.arange(slot_count, dtype=jnp.int32)[None, :] < leaf_counts[:, None]
     block_live = jnp.any((leaf_rows == my_block) & active_slots, axis=1)
     targets = jnp.arange(ROW_DEV, dtype=jnp.int32)
-    top_strip = lax.all_gather(top_inverse, "col", axis=2, tiled=True)
+    top_strip = set_side(top_inverse, 2)
     section = lax.all_gather(panel, "row", axis=1, tiled=True)
     length = section.shape[1]
     gains_prod = []

time: 627 us -> 633 us (level)
  waiting for transfers between devices: 500 us -> 477 us
  local copies, waits for them, and re-layouts: 35.5 us -> 54.2 us
  starting transfers between devices: 0.12 us -> 9.44 us
    all_gather x1, waiting for transfers between devices: 103 us -> 15.4 us  [on_device(): section = lax.all_gather(panel, 'row', axis=1, tiled=True)]
    all_to_all x0 -> x1, waiting for transfers between devices: none -> 60 us  [jax.lax.all_to_all(jnp.stack([my_data for _ in range(jax.lax.axis_size('c...]
    psum x1, waiting for transfers between devices: 343 us -> 401 us  [on_device(): total_sum = lax.psum(partial_diag, 'row')]
    all_gather x1 -> x0, waiting for transfers between devices: 52.9 us -> none  [on_device(): top_strip = lax.all_gather(top_inverse, 'col', axis=2, tiled=True)]
    reshape x0 -> x1, local copies, waits for them, and re-layouts: none -> 16.2 us  [jnp.concatenate(jax.lax.all_to_all(jnp.stack([my_data for _ in range(jax....]
    all_to_all x0 -> x1, starting transfers between devices: none -> 9.36 us  [jax.lax.all_to_all(jnp.stack([my_data for _ in range(jax.lax.axis_size('c...]
  transfers between devices with their start and end apart: 3 -> 3, of which waited for: 3 -> 3; matrix products, arithmetic and copies ran while one was open for 13% -> 15% of each run, Pallas kernels for 0% -> 0%
where the time goes in v1:
time: 633 us; the launch traced here: 632 us
  waiting for transfers between devices  477 us (75%)
  local copies, waits for them, and re-layouts  54.2 us (9%)
  other arithmetic  54.2 us (9%)
  matrix products  22.6 us (4%)
  between operations  14.4 us (2%)
  starting transfers between devices  9.44 us (1%)
    psum x1, waiting for transfers between devices, on_device(): total_sum = lax.psum(partial_diag, 'row')  401 us
    all_to_all x1, waiting for transfers between devices, jax.lax.all_to_all(jnp.stack([my_data for _ in range(jax.lax.axis_size('c...  60 us
    gather x2, local copies, waits for them, and re-layouts, on_device(): picked = jnp.take(top_strip, columns, axis=2)  25.5 us
    dot_general x20, matrix products, product_highest(): jnp.dot(left, right, precision=lax.Precision.HIGHEST, preferred_element_t...  22.6 us
    reshape x1, local copies, waits for them, and re-layouts, jnp.concatenate(jax.lax.all_to_all(jnp.stack([my_data for _ in range(jax....  16.2 us
    all_gather x1, waiting for transfers between devices, on_device(): section = lax.all_gather(panel, 'row', axis=1, tiled=True)  15.4 us
    select_n x2, other arithmetic, on_device(): picked = jnp.take(top_strip, columns, axis=2)  14.9 us
  transfers between devices with their start and end apart: 3, of which 3 were waited for; matrix products, arithmetic and copies ran while one was open for 15% of the time, Pallas kernels for 0%

profile of v1, /device:TPU:1, one launch (start us, length us, event | category | flops | bytes accessed | tf_op | source)
XLA Modules:
  0.0 631.9 jit_solution(2056240660681575497)
XLA Ops:
  7.2 1.1 copy.14
  8.2 2.4 stack.26
  10.6 9.4 %all-to-all-start = ((f32[16,2,128,256]{2,3,1,0:T(8,128)}), f32[16,2,128,256]{2,3,1,0:T(8,128)}, u32[]{:S(2)}, u32[]{:S(2)}) async-start(f32[16,2,128,256]{2,3,1,0:T(8,128)} %stack.26), calls=%async_computation | async-start | bytes 8388608 | tf_op jit(solution)/shard_map/all_to_all | solution.py:10
  20.0 0.0 all-gather.2.cloned.1.call-start
  20.1 0.7 all-gather.2.cloned.1.call-update
  20.8 0.0 all-reduce.2.cloned.1.call-start
  20.8 0.0 copy-done.4
  20.8 0.0 copy-done.5
  20.8 0.2 and_reduce_fusion
  21.0 0.1 broadcast_bitcast_fusion
  21.1 0.7 fusion.70
  21.8 5.0 compare_and_fusion.1
  26.9 0.6 fusion.69
  27.5 5.6 compare_and_fusion.3
  33.1 5.0 compare_and_fusion
  38.2 5.7 compare_and_fusion.2
  43.8 5.0 broadcast_clamp_fusion
  48.9 5.0 broadcast_clamp_fusion.1
  53.9 1.2 fusion.65
  55.2 60.0 %all-to-all-done = f32[16,2,128,256]{2,3,1,0:T(8,128)} async-done(((f32[16,2,128,256]{2,3,1,0:T(8,128)}), f32[16,2,128,256]{2,3,1,0:T(8,128)}, u32[]{:S(2)}, u32[]{:S(2)}) %all-to-all-start) | async-done | bytes 4194336 | tf_op jit(solution)/shard_map/all_to_all | solution.py:10
  115.1 2.5 copy.15
  117.6 16.2 %copy.16 = f32[2,128,4096]{1,0,2:T(2,128)} copy(f32[2,128,4096]{1,2,0:T(8,128)S(1)} %bitcast.120) | data formatting | bytes 8388608 | tf_op jit(solution)/shard_map/reshape | solution.py:9
  133.8 9.0 %gather_fusion.1 = f32[2048,2,128]{2,1,0:T(2,128)S(1)} fusion(f32[2,128,4096]{1,0,2:T(2,128)} %copy.16, s32[2048]{0:T(1024)S(1)} %broadcast_clamp_fusion), kind=kCustom, calls=%fused_computation.1.clone | custom fusion | bytes 4202496 | tf_op jit(solution)/shard_map/jit(_take)/gather | solution.py:50
  142.8 16.6 %gather_fusion = f32[2048,2,128]{2,1,0:T(2,128)} fusion(f32[2,128,4096]{1,0,2:T(2,128)} %copy.16, s32[2048]{0:T(1024)S(1)} %broadcast_clamp_fusion.1), kind=kCustom, calls=%fused_computation.clone | custom fusion | bytes 4202496 | tf_op jit(solution)/shard_map/jit(_take)/gather | solution.py:50
  159.3 7.4 %select_bitcast_fusion = f32[2,128,2048]{1,0,2:T(2,128)S(1)} fusion(f32[2048,2,128]{2,1,0:T(2,128)S(1)} %gather_fusion.1, pred[2048]{0:T(1024)(128)(4,1)S(1)} %compare_and_fusion), kind=kLoop, calls=%fused_computation.8 | loop fusion | flops 524288 | bytes 4196352 | tf_op jit(solution)/shard_map/jit(_take)/select_n | solution.py:50
  166.8 0.0 copy-start.1
  166.8 1.7 fusion.68
  168.4 0.1 copy-done.1
  168.5 7.4 %select_bitcast_fusion.1 = f32[2,128,2048]{1,0,2:T(2,128)S(1)} fusion(f32[2048,2,128]{2,1,0:T(2,128)S(1)} %copy-done.1, pred[2048]{0:T(1024)(128)(4,1)S(1)} %compare_and_fusion.1), kind=kLoop, calls=%fused_computation.9 | loop fusion | flops 524288 | bytes 4196352 | tf_op jit(solution)/shard_map/jit(_take)/select_n | solution.py:50
  175.9 2.5 fusion.67
  178.4 15.4 %all-gather.2.cloned.1.call-done = f32[2,2048,512]{2,1,0:T(8,128)} async-done(((f32[2,64,512]{2,1,0:T(8,128)}), f32[2,2048,512]{2,1,0:T(8,128)}) %all-gather.2.cloned.1.call-update) | async-done | bytes 8388624 | tf_op jit(solution)/shard_map/all_gather | solution.py:35
  193.8 4.1 slice_multiply_fusion.1
  197.9 1.0 fusion.3
  198.9 1.0 fusion
  199.9 1.0 fusion.9
  201.0 1.0 fusion.6
  202.0 0.0 copy-start
  202.0 1.9 fusion.1
  203.9 0.0 copy-done
  203.9 1.9 fusion.2
  205.8 1.9 fusion.23
  207.8 1.9 fusion.21
  209.6 2.1 fusion.7
  211.7 1.9 fusion.8
  213.6 1.9 fusion.19
  215.4 1.9 fusion.17
  217.3 0.1 fusion.30
  217.4 0.0 copy-start.2
  217.4 0.4 fusion.41
  217.8 0.4 fusion.42
  218.2 0.4 fusion.12
  218.6 0.4 fusion.13
  219.1 0.4 fusion.39
  219.5 0.4 fusion.40
  219.9 0.4 fusion.14
  220.3 0.0 copy-done.2
  220.3 0.0 copy-start.3
  220.3 0.4 fusion.15
  220.8 1.1 maximum_maximum_fusion
  221.8 0.0 all-reduce.2.cloned.1.call-update
  221.9 0.2 copy.18
  222.1 400.9 %all-reduce.2.cloned.1.call-done = f32[2,256,512]{1,2,0:T(8,128)} async-done(((f32[2,256,512]{1,2,0:T(8,128)}), f32[2,256,512]{1,2,0:T(8,128)}) %all-reduce.2.cloned.1.call-update) | async-done | bytes 1048592 | tf_op jit(solution)/shard_map/psum | solution.py:75
  623.0 1.2 dynamic-slice_subtract_fusion
  624.3 0.8 copy.19
  (7 shorter events, 0.0 us)
Async XLA Ops:
  10.6 10.2 %copy-start.4 = (s32[2]{0:T(128)S(1)}, s32[2]{0:T(128)}, u32[]{:S(2)}) copy-start(s32[2]{0:T(128)} %param.12) | copy-start | bytes 28
  10.6 10.2 %copy-start.5 = (s32[2,8]{1,0:T(2,128)S(1)}, s32[2,8]{1,0:T(2,128)}, u32[]{:S(2)}) copy-start(s32[2,8]{1,0:T(2,128)} %param.11) | copy-start | bytes 196
  10.6 104.5 %all-to-all-start = ((f32[16,2,128,256]{2,3,1,0:T(8,128)}), f32[16,2,128,256]{2,3,1,0:T(8,128)}, u32[]{:S(2)}, u32[]{:S(2)}) async-start(f32[16,2,128,256]{2,3,1,0:T(8,128)} %stack.26), calls=%async_computation | async-start | bytes 8388608 | tf_op jit(solution)/shard_map/all_to_all | solution.py:10
  20.0 173.8 %all-gather.2.cloned.1.call-start = ((), (), s32[]{:S(2)}) async-start(), calls=%async_computation.1 | async-start | bytes 8650752 | tf_op jit(solution)/shard_map/all_gather | solution.py:35
  20.8 602.3 %all-reduce.2.cloned.1.call-start = ((), (), s32[]{:S(2)}) async-start(), calls=%async_computation.2 | async-start | bytes 2097152 | tf_op jit(solution)/shard_map/psum | solution.py:75
  166.8 1.7 copy-start.1
  202.0 1.9 copy-start
  217.4 3.0 copy-start.2
  220.3 1.5 copy-start.3
Sparse Core Ops, SparseCore 0:
  24.1 169.6 all-gather.1
  222.0 400.9 all-reduce.1
